TPU v7x, 32 devices: a whole 2x2x4 slice. The times are simulated.
32 devices in a mesh: group: 2 (over y), clip: 4 (over z), pix: 4 (over x, core).
Axes of the slice: x: 2, y: 2, z: 4, core: 2. Of those that a mesh axis runs over, the one named last changes fastest.
Arguments:
- latents: bfloat16 [64, 256, 320], P(('group', 'clip'), 'pix'), parts along dimension 0, may hold values from -6 to 6
- sampled: int32 [8], P(('group', 'clip')), parts along dimension 0, may hold values from 0 to 7
- temporal_gain: float32 [320], replicated, may hold values from 0.5 to 1.5
- temporal_qkv: bfloat16 [320, 960], replicated, may hold values from -64 to 64
- temporal_out: bfloat16 [320, 320], replicated, may hold values from -0.3125 to 0.3125
- spatial_gain: float32 [320], replicated, may hold values from 0.5 to 1.5
- spatial_qkv: bfloat16 [320, 960], replicated, may hold values from -64 to 64
- spatial_out: bfloat16 [320, 320], replicated, may hold values from -0.3125 to 0.3125
Outputs:
- refined: bfloat16 [64, 256, 320], P(('group', 'clip', 'pix')), parts along dimension 0
There are 2 independent parts, one for each index of `group`. A program takes and returns all parts, laid end to end along the dimension named above; an argument that names none is the same for every part. Nothing has to cross between parts.
All inputs are finite; a program needn't handle non-finite values.
Results may differ from a plain program's by a relative error of at most 0.014.
The roundings to bfloat16 on the way count: a program that leaves them out, or rounds other values in their place, can miss the bound.
Values may be sent and summed in bfloat16 or wider, within the bound.
No kernel may reach another device: no remote copies, remote signals or barrier semaphores. Data moves between devices by JAX's collectives and lax.ppermute only.
A program may use at most 64 MiB of HBM per device.

v0:
```python
import math
import jax
import jax.numpy as jnp
from jax import lax
from jax.sharding import PartitionSpec as P

HEADS = 5
HEAD_DIM = 64
HALO = 4


def with_halo(block, sides, width):
    for axis, dim in sides:
        count = lax.axis_size(axis)
        forward = [(i, i + 1) for i in range(count - 1)]
        backward = [(target, source) for source, target in forward]
        low = lax.ppermute(
            lax.slice_in_dim(block, block.shape[dim] - width, None, axis=dim), axis, forward
        )
        high = lax.ppermute(lax.slice_in_dim(block, 0, width, axis=dim), axis, backward)
        block = jnp.concatenate([low, block, high], axis=dim)
    return block


def layer_norm(frame_rows, scales):
    values = frame_rows.astype(jnp.float32)
    average = jnp.mean(values, axis=-1, keepdims=True)
    centred = values - average
    spread = jnp.mean(centred * centred, axis=-1, keepdims=True)
    return (centred * lax.rsqrt(spread + 1e-05) * scales).astype(jnp.bfloat16)


def project(frame_rows, matrix):
    shape = frame_rows.shape
    flat = frame_rows.reshape(-1, shape[-1])
    result = jnp.dot(flat, matrix, preferred_element_type=jnp.float32).astype(jnp.bfloat16)
    return result.reshape(shape[:-1] + (matrix.shape[1],))


def temporal_attend(queries, key_pairs, usable):
    count, pixels, channels = queries.shape
    depth = key_pairs.shape[0]
    keys = key_pairs[..., :channels].reshape(depth, pixels, HEADS, HEAD_DIM)
    values = key_pairs[..., channels:].reshape(depth, pixels, HEADS, HEAD_DIM)
    query_heads = queries.reshape(count, pixels, HEADS, HEAD_DIM)
    scores = jnp.einsum(
        "fphd,kphd->phfk", query_heads, keys, preferred_element_type=jnp.float32
    ) / math.sqrt(HEAD_DIM)
    scores = jnp.where(usable[None, None, None, :], scores, -1e30)
    highest = jnp.max(scores, axis=-1, keepdims=True)
    expo = jnp.exp(scores - highest)
    weights = (expo / jnp.sum(expo, axis=-1, keepdims=True)).astype(jnp.bfloat16)
    mixed = jnp.einsum("phfk,kphd->fphd", weights, values, preferred_element_type=jnp.float32)
    return mixed.reshape(count, pixels, channels).astype(jnp.bfloat16)


def spatial_frame(frame_rows, scales, qkv_matrix, out_matrix):
    pixels, channels = frame_rows.shape
    normed = layer_norm(frame_rows, scales)
    packed = jnp.dot(normed, qkv_matrix, preferred_element_type=jnp.float32).astype(jnp.bfloat16)
    heads_view = packed.reshape(pixels, 3, HEADS, HEAD_DIM).transpose(1, 2, 0, 3)
    block_rows = 512 if pixels % 512 == 0 else pixels

    def one_head(triple):
        queries, keys, values = triple

        def query_block(query_rows):
            scores = jnp.dot(query_rows, keys.T, preferred_element_type=jnp.float32) / math.sqrt(
                HEAD_DIM
            )
            highest = jnp.max(scores, axis=-1, keepdims=True)
            expo = jnp.exp(scores - highest)
            weights = (expo / jnp.sum(expo, axis=-1, keepdims=True)).astype(jnp.bfloat16)
            return jnp.dot(weights, values, preferred_element_type=jnp.float32).astype(jnp.bfloat16)

        blocks = lax.map(query_block, queries.reshape(pixels // block_rows, block_rows, HEAD_DIM))
        return blocks.reshape(pixels, HEAD_DIM)

    mixed = lax.map(one_head, (heads_view[0], heads_view[1], heads_view[2]))
    mixed = mixed.transpose(1, 0, 2).reshape(pixels, channels)
    update = jnp.dot(mixed, out_matrix, preferred_element_type=jnp.float32)
    return (frame_rows.astype(jnp.float32) + update).astype(jnp.bfloat16)


def body(
    latents,
    sampled,
    temporal_gain,
    temporal_qkv,
    temporal_out,
    spatial_gain,
    spatial_qkv,
    spatial_out,
):
    frames_here, pixel_count, channels = latents.shape
    normed = layer_norm(latents, temporal_gain)
    queries = project(normed, temporal_qkv[:, :channels])
    pair_matrix = temporal_qkv[:, channels:]
    picked = lax.dynamic_slice_in_dim(normed, sampled[0], 1, 0)
    global_pairs = project(lax.all_gather(picked, "clip", axis=0, tiled=True), pair_matrix)
    border_rows = with_halo(normed, (("clip", 0),), HALO)
    border = project(border_rows, pair_matrix)
    clip_index = lax.axis_index("clip")
    clip_count = lax.axis_size("clip")
    positions = (
        clip_index * frames_here - HALO + jnp.arange(frames_here + 2 * HALO, dtype=jnp.int32)
    )
    inside = (positions >= 0) & (positions < clip_count * frames_here)
    usable = jnp.concatenate([inside, jnp.ones((global_pairs.shape[0],), jnp.bool_)])
    attended = temporal_attend(queries, jnp.concatenate([border, global_pairs], 0), usable)
    update = jnp.dot(
        attended.reshape(-1, channels), temporal_out, preferred_element_type=jnp.float32
    )
    temporal_rows = (latents.astype(jnp.float32).reshape(-1, channels) + update).astype(
        jnp.bfloat16
    )
    pix_count = lax.axis_size("pix")
    per_device = frames_here // pix_count
    grouped = temporal_rows.reshape(pix_count, per_device, pixel_count, channels)
    frame_block = lax.all_to_all(grouped, "pix", split_axis=0, concat_axis=2, tiled=True)[0]
    result = lax.map(
        lambda frame_rows: spatial_frame(frame_rows, spatial_gain, spatial_qkv, spatial_out),
        frame_block,
    )
    whole = result[None]
    return whole.reshape(whole.shape[1], whole.shape[2], channels)


def solution(mesh):
    placed = (P(("group", "clip"), "pix", None), P(("group", "clip")), P(), P(), P(), P(), P(), P())
    return jax.shard_map(
        body,
        mesh=mesh,
        in_specs=placed,
        out_specs=P(("group", "clip", "pix"), None, None),
        check_vma=False,
    )
```

profile of v0, /device:TPU:0, one launch (start us, length us, event | category | flops | bytes accessed | tf_op | source)
XLA Modules:
  0.0 77.4 jit_solution(4738823542584057212)
XLA Ops:
  0.0 1.2 %convert_reduce_fusion.1 = f32[8,64]{1,0:T(8,128)S(1)} fusion(bf16[8,64,320]{2,1,0:T(8,128)(2,1)} %param.12), kind=kLoop, calls=%fused_computation.59 | loop fusion | flops 327168 | bytes 329728 | tf_op jit(solution)/shard_map/reduce_sum | solution.py:27
  1.2 1.3 %multiply_reduce_fusion = f32[8,64]{1,0:T(8,128)S(1)} fusion(bf16[8,64,320]{2,1,0:T(8,128)(2,1)} %param.12, f32[8,64]{1,0:T(8,128)S(1)} %broadcast_multiply_fusion.1), kind=kLoop, calls=%fused_computation.57 | loop fusion | flops 654848 | bytes 331776 | tf_op jit(solution)/shard_map/reduce_sum | solution.py:29
  2.5 1.2 %multiply_convert_fusion = bf16[8,64,320]{2,1,0:T(8,128)(2,1)S(1)} fusion(bf16[8,64,320]{2,1,0:T(8,128)(2,1)} %param.12, f32[320]{0:T(512)} %param.14, f32[8,64]{1,0:T(8,128)S(1)} %add_rsqrt_fusion.1, f32[8,64]{1,0:T(8,128)S(1)} %broadcast_multiply_fusion.1), kind=kLoop, calls=%fused_computation.56 | loop fusion | flops 819200 | bytes 660736 | tf_op jit(solution)/shard_map/convert_element_type | solution.py:30
  3.7 0.8 %fusion.38 = (bf16[4,64,320]{2,1,0:T(8,128)(2,1)}, bf16[4,64,320]{2,1,0:T(8,128)(2,1)}) fusion(bf16[8,64,320]{2,1,0:T(8,128)(2,1)S(1)} %multiply_convert_fusion), kind=kLoop, calls=%fused_computation.68 | loop fusion | bytes 655360 | tf_op jit(solution)/shard_map/slice | solution.py:18
  4.5 5.0 %collective-permute-start = (bf16[4,64,320]{2,1,0:T(8,128)(2,1)}, bf16[4,64,320]{2,1,0:T(8,128)(2,1)S(1)}, u32[]{:S(2)}, u32[]{:S(2)}) collective-permute-start(bf16[4,64,320]{2,1,0:T(8,128)(2,1)} %get-tuple-element.121), channel_id=1, source_target_pairs={{0,4},{4,8},{8,12},{1,5},{5,9},{9,13},{2,6},{6,10},{10,14},{3,7},{... | collective-permute-start | bytes 491528 | tf_op jit(solution)/shard_map/ppermute | solution.py:17
  9.5 1.3 %collective-permute-start.1 = (bf16[4,64,320]{2,1,0:T(8,128)(2,1)}, bf16[4,64,320]{2,1,0:T(8,128)(2,1)}, u32[]{:S(2)}, u32[]{:S(2)}) collective-permute-start(bf16[4,64,320]{2,1,0:T(8,128)(2,1)} %get-tuple-element.122), channel_id=1, source_target_pairs={{4,0},{8,4},{12,8},{5,1},{9,5},{13,9},{6,2},{10,6},{14,10},{7,3},{... | collective-permute-start | bytes 491528 | tf_op jit(solution)/shard_map/ppermute | solution.py:20
  11.5 16.6 %all_gather.3 = bf16[4,64,320]{2,1,0:T(8,128)(2,1)S(1)} all-gather(bf16[1,64,320]{2,1,0:T(8,128)(2,1)S(1)} %constant_dynamic-slice_fusion), channel_id=1, replica_groups=mesh['group'=2,'clip'=4,'pix'=4] {'clip'}, dimensions={0}, use_global_device_ids=true | all-gather | bytes 204800 | tf_op jit(solution)/shard_map/all_gather | solution.py:100
  28.5 0.5 convolution_convert_fusion.5
  28.9 1.1 %copy.26 = bf16[4,64,640]{1,2,0:T(8,128)(2,1)} copy(bf16[4,64,640]{2,1,0:T(8,128)(2,1)S(1)} %bitcast.127) | data formatting | bytes 655360 | tf_op jit(solution)/shard_map/reshape | solution.py:37
  30.4 0.6 copy.27
  31.0 1.0 %copy.31 = f32[512,320]{0,1:T(8,128)} copy(bf16[512,320]{1,0:T(8,128)(2,1)S(1)} %bitcast.121) | data formatting | bytes 983040 | tf_op jit(solution)/shard_map/reshape | solution.py:114
  32.0 1.1 %pad_maximum_fusion.1 = bf16[16,64,320]{2,1,0:T(8,128)(2,1)S(1)} fusion(bf16[4,64,320]{2,1,0:T(8,128)(2,1)} %collective-permute-done.1, bf16[8,64,320]{2,1,0:T(8,128)(2,1)S(1)} %multiply_convert_fusion, bf16[4,64,320]{2,1,0:T(8,128)(2,1)S(1)} %collective-permute-done), kind=kLoop, calls=%fused_computation.55 | loop fusion | flops 655360 | bytes 1310720 | tf_op jit(solution)/shard_map/concatenate | solution.py:21
  33.1 2.0 %convolution_convert_fusion.2 = bf16[1024,640]{1,0:T(8,128)(2,1)} fusion(bf16[1024,320]{1,0:T(8,128)(2,1)S(1)} %bitcast.124, bf16[320,960]{1,0:T(8,128)(2,1)S(1)} %copy-done.5), kind=kOutput, calls=%fused_computation.43 | convolution fusion | flops 420085760 | bytes 2506752 | tf_op jit(solution)/shard_map/dot_general | solution.py:36
  35.1 3.2 %copy.25 = bf16[16,64,640]{1,2,0:T(8,128)(2,1)S(1)} copy(bf16[16,64,640]{2,1,0:T(8,128)(2,1)} %bitcast.122) | data formatting | bytes 2621440 | tf_op jit(solution)/shard_map/reshape | solution.py:37
  38.4 3.6 %pad_maximum_fusion = (bf16[20,64,320]{1,2,0:T(8,128)(2,1)}, bf16[20,64,320]{1,2,0:T(8,128)(2,1)}) fusion(bf16[4,64,640]{1,2,0:T(8,128)(2,1)} %copy.26, bf16[16,64,640]{1,2,0:T(8,128)(2,1)S(1)} %copy.25), kind=kLoop, calls=%fused_computation.42 | loop fusion | flops 3276800 | bytes 3276800 | tf_op jit(solution)/shard_map/concatenate | solution.py:110
  42.0 2.9 %copy.28 = bf16[20,64,5,64]{3,0,2,1:T(8,128)(2,1)S(1)} copy(bf16[20,64,5,64]{1,3,2,0:T(8,128)(2,1)} %bitcast.120) | data formatting | bytes 1638400 | tf_op jit(solution)/shard_map/reshape | solution.py:43
  45.0 3.9 %copy.29 = bf16[20,64,5,64]{3,0,2,1:T(8,128)(2,1)} copy(bf16[20,64,5,64]{1,3,2,0:T(8,128)(2,1)} %bitcast.119) | data formatting | bytes 1638400 | tf_op jit(solution)/shard_map/reshape | solution.py:44
  48.8 2.3 %fusion.39 = (f32[64,5,8]{2,1,0:T(8,128)S(1)}, f32[64,5,8,20]{3,2,1,0:T(8,128)}) fusion(bf16[8,64,5,64]{3,0,2,1:T(8,128)(2,1)S(1)} %copy.27, bf16[20,64,5,64]{3,0,2,1:T(8,128)(2,1)S(1)} %copy.28, pred[20]{0:T(512)(128)(4,1)S(1)} %concatenate.11), kind=kOutput, calls=%fused_computation.69 | convolution fusion | flops 6758419 | bytes 1361940 | tf_op jit(solution)/shard_map/sub | solution.py:51
  51.1 2.7 %fusion.31 = bf16[8,64,5,64]{3,0,2,1:T(8,128)(2,1)S(1)} fusion(bf16[20,64,5,64]{3,0,2,1:T(8,128)(2,1)} %copy.29, f32[64,5,8,20]{3,2,1,0:T(8,128)} %get-tuple-element.124, f32[64,5,8]{2,1,0:T(8,128)S(1)} %get-tuple-element.123), kind=kOutput, calls=%fused_computation.50 | convolution fusion | flops 6819840 | bytes 1361920 | tf_op jit(solution)/shard_map/phfk,kphd->fphd/dot_general | solution.py:53
  53.8 0.6 copy.30
  55.3 0.9 %copy.32 = bf16[512,320]{1,0:T(8,128)(2,1)} copy(bf16[512,320]{0,1:T(8,128)(2,1)S(1)} %fusion.32) | data formatting | bytes 655360 | tf_op jit(solution)/shard_map/convert_element_type | solution.py:114
  56.2 3.5 %all-to-all-start = ((bf16[4,2,64,320]{3,2,1,0:T(8,128)(2,1)}), bf16[4,2,64,320]{3,2,1,0:T(8,128)(2,1)S(1)}, u32[]{:S(2)}, u32[]{:S(2)}) async-start(bf16[4,2,64,320]{3,2,1,0:T(8,128)(2,1)} %bitcast.23), calls=%async_computation | async-start | bytes 786432 | tf_op jit(solution)/shard_map/all_to_all | solution.py:120
  59.7 7.4 %all-to-all-done = bf16[4,2,64,320]{3,2,1,0:T(8,128)(2,1)S(1)} async-done(((bf16[4,2,64,320]{3,2,1,0:T(8,128)(2,1)}), bf16[4,2,64,320]{3,2,1,0:T(8,128)(2,1)S(1)}, u32[]{:S(2)}, u32[]{:S(2)}) %all-to-all-start) | async-done | bytes 327712 | tf_op jit(solution)/shard_map/all_to_all | solution.py:120
  67.3 10.0 %while.25 = (s32[]{:T(128)}, bf16[2,256,320]{1,2,0:T(8,128)(2,1)}, bf16[2,256,320]{1,2,0:T(8,128)(2,1)S(1)}, f32[320]{0:T(512)S(1)}, bf16[320,960]{1,0:T(8,128)(...) while((s32[]{:T(128)}, bf16[2,256,320]{1,2,0:T(8,128)(2,1)}, ...), condition=%wide.region_11.12_spmd, body=%wide.region_4.11_spmd.sunk | while | flops 228359936 | bytes 7997730 | solution.py:121
  67.5 0.5 convolution_convert_fusion.7
  68.1 0.5 copy.36
  68.7 2.6 %while.26 = (s32[]{:T(128)}, bf16[5,256,64]{1,2,0:T(8,128)(2,1)S(1)}, bf16[5,256,64]{2,1,0:T(8,128)(2,1)S(1)}, bf16[5,256,64]{2,1,0:T(8,128)(2,1)S(1)}, bf16[5,256,64]{2,1,0:T(8,128)(2,1)S(1)}, /*index=5*/s32[]{:T(128)}) while((s32[]{:T(128)}, bf16[5,256,64]{1,2,0:T(8,128)(2,1)S(1)}, bf16[5,256,64]{2,1,0:T(8,128)(2,1)S(1)}, ...), condition=%wide.region_10.10_spmd, body=%wide.region_7.9_spmd.sunk | while | flops 17251840 | bytes 1023045 | solution.py:79
  71.6 0.7 copy-done.8
  72.5 0.5 convolution_convert_fusion.7
  73.1 0.5 copy.36
  73.7 2.6 %while.26 = (s32[]{:T(128)}, bf16[5,256,64]{1,2,0:T(8,128)(2,1)S(1)}, bf16[5,256,64]{2,1,0:T(8,128)(2,1)S(1)}, bf16[5,256,64]{2,1,0:T(8,128)(2,1)S(1)}, bf16[5,256,64]{2,1,0:T(8,128)(2,1)S(1)}, /*index=5*/s32[]{:T(128)}) while((s32[]{:T(128)}, bf16[5,256,64]{1,2,0:T(8,128)(2,1)S(1)}, bf16[5,256,64]{2,1,0:T(8,128)(2,1)S(1)}, ...), condition=%wide.region_10.10_spmd, body=%wide.region_7.9_spmd.sunk | while | flops 17251840 | bytes 1023045 | solution.py:79
  76.6 0.7 copy-done.8
  (78 shorter events, 8.0 us)
Async XLA Ops:
  0.0 54.8 %copy-start = (bf16[320,320]{1,0:T(8,128)(2,1)S(1)}, bf16[320,320]{1,0:T(8,128)(2,1)}, u32[]{:S(2)}) copy-start(bf16[320,320]{1,0:T(8,128)(2,1)} %param.16) | copy-start | bytes 614404
  0.0 28.1 %copy-start.5 = (bf16[320,960]{1,0:T(8,128)(2,1)S(1)}, bf16[320,960]{1,0:T(8,128)(2,1)}, u32[]{:S(2)}) copy-start(bf16[320,960]{1,0:T(8,128)(2,1)} %param.15) | copy-start | bytes 1843204
  4.5 27.5 %collective-permute-start = (bf16[4,64,320]{2,1,0:T(8,128)(2,1)}, bf16[4,64,320]{2,1,0:T(8,128)(2,1)S(1)}, u32[]{:S(2)}, u32[]{:S(2)}) collective-permute-start(bf16[4,64,320]{2,1,0:T(8,128)(2,1)} %get-tuple-element.121), channel_id=1, source_target_pairs={{0,4},{4,8},{8,12},{1,5},{5,9},{9,13},{2,6},{6,10},{10,14},{3,7},{... | collective-permute-start | bytes 491528 | tf_op jit(solution)/shard_map/ppermute | solution.py:17
  9.5 22.5 %collective-permute-start.1 = (bf16[4,64,320]{2,1,0:T(8,128)(2,1)}, bf16[4,64,320]{2,1,0:T(8,128)(2,1)}, u32[]{:S(2)}, u32[]{:S(2)}) collective-permute-start(bf16[4,64,320]{2,1,0:T(8,128)(2,1)} %get-tuple-element.122), channel_id=1, source_target_pairs={{4,0},{8,4},{12,8},{5,1},{9,5},{13,9},{6,2},{10,6},{14,10},{7,3},{... | collective-permute-start | bytes 491528 | tf_op jit(solution)/shard_map/ppermute | solution.py:20
  28.9 2.0 %copy-start.2 = (bf16[8,64,320]{2,1,0:T(8,128)(2,1)S(1)}, bf16[8,64,320]{2,1,0:T(8,128)(2,1)}, u32[]{:S(2)}) copy-start(bf16[8,64,320]{2,1,0:T(8,128)(2,1)} %param.12) | copy-start | bytes 983044
  53.8 1.1 %copy-start.4 = (f32[512,320]{0,1:T(8,128)S(1)}, f32[512,320]{0,1:T(8,128)}, u32[]{:S(2)}) copy-start(f32[512,320]{0,1:T(8,128)} %copy.31) | copy-start | bytes 1966084
  55.3 12.0 %copy-start.1 = (bf16[320,960]{1,0:T(8,128)(2,1)S(1)}, bf16[320,960]{1,0:T(8,128)(2,1)}, u32[]{:S(2)}) copy-start(bf16[320,960]{1,0:T(8,128)(2,1)} %param.18) | copy-start | bytes 1843204
  55.3 12.0 %copy-start.3 = (bf16[320,320]{1,0:T(8,128)(2,1)S(1)}, bf16[320,320]{1,0:T(8,128)(2,1)}, u32[]{:S(2)}) copy-start(bf16[320,320]{1,0:T(8,128)(2,1)} %param.19) | copy-start | bytes 614404
  55.3 12.0 %copy-start.6 = (f32[320]{0:T(512)S(1)}, f32[320]{0:T(512)}, u32[]{:S(2)}) copy-start(f32[320]{0:T(512)} %param.17) | copy-start | bytes 3844
  56.2 10.8 %all-to-all-start = ((bf16[4,2,64,320]{3,2,1,0:T(8,128)(2,1)}), bf16[4,2,64,320]{3,2,1,0:T(8,128)(2,1)S(1)}, u32[]{:S(2)}, u32[]{:S(2)}) async-start(bf16[4,2,64,320]{3,2,1,0:T(8,128)(2,1)} %bitcast.23), calls=%async_computation | async-start | bytes 786432 | tf_op jit(solution)/shard_map/all_to_all | solution.py:120
  68.6 2.7 %copy-start.7 = (bf16[2,256,320]{1,2,0:T(8,128)(2,1)S(1)}, bf16[2,256,320]{1,2,0:T(8,128)(2,1)}, u32[]{:S(2)}) copy-start(bf16[2,256,320]{1,2,0:T(8,128)(2,1)} %get-tuple-element.244) | copy-start | bytes 983044 | tf_op jit(solution)/shard_map/while
  71.6 0.7 copy-start.8
  73.6 2.7 %copy-start.7 = (bf16[2,256,320]{1,2,0:T(8,128)(2,1)S(1)}, bf16[2,256,320]{1,2,0:T(8,128)(2,1)}, u32[]{:S(2)}) copy-start(bf16[2,256,320]{1,2,0:T(8,128)(2,1)} %get-tuple-element.244) | copy-start | bytes 983044 | tf_op jit(solution)/shard_map/while
  76.6 0.7 copy-start.8
where the time goes:
time: 77.9 us; the launch traced here: 77.4 us
  local copies, waits for them, and re-layouts  18.6 us (24%)
  blocking collectives  16.6 us (21%)
  matrix products  14.3 us (18%)
  starting transfers between devices  9.71 us (12%)
  other arithmetic  9.49 us (12%)
  waiting for transfers between devices  7.37 us (9%)
  between operations  0.92 us (1%)
    all_gather x1, blocking collectives, body(): lax.all_gather(picked, 'clip', axis=0, tiled=True)  16.6 us
    all_to_all x1, waiting for transfers between devices, body(): lax.all_to_all(grouped, 'pix', split_axis=0, concat_axis=2, tiled=True)[0]  7.37 us
    ppermute x1, starting transfers between devices, with_halo(): lax.ppermute(lax.slice_in_dim(block, block.shape[dim] - width, None, axis...  4.96 us
    reshape x2, local copies, waits for them, and re-layouts, project(): return result.reshape(shape[:-1] + (matrix.shape[1],))  4.31 us
    reshape x1, local copies, waits for them, and re-layouts, temporal_attend(): values = key_pairs[..., channels:].reshape(depth, pixels, HEADS, HEAD_DIM)  3.85 us
    concatenate x1, other arithmetic, body(): jnp.concatenate([border, global_pairs], 0)  3.64 us
    all_to_all x1, starting transfers between devices, body(): lax.all_to_all(grouped, 'pix', split_axis=0, concat_axis=2, tiled=True)[0]  3.46 us
    reshape x1, local copies, waits for them, and re-layouts, temporal_attend(): keys = key_pairs[..., :channels].reshape(depth, pixels, HEADS, HEAD_DIM)  2.93 us
  transfers between devices with their start and end apart: 3, of which 1 were waited for; matrix products, arithmetic and copies ran while one was open for 5% of the time, Pallas kernels for 0%

commit v1 on v0

--- a/solution.py
+++ b/solution.py
@@ -1,3 +1,4 @@
+import functools
 import math
 import jax
 import jax.numpy as jnp
@@ -7,6 +8,37 @@
 HEADS = 5
 HEAD_DIM = 64
 HALO = 4
+
+
+def _remake_run(payload, dim_k, chunk):
+    answer = payload.shape
+    return jnp.moveaxis(
+        payload.reshape(*answer[:dim_k], chunk, answer[dim_k] // chunk, *answer[dim_k + 1 :]),
+        dim_k,
+        0,
+    )
+
+
+def _clear_levels_all(tile_in, out_dim):
+    wide_out = list(tile_in.shape[1:])
+    wide_out[out_dim] *= tile_in.shape[0]
+    return jnp.moveaxis(tile_in, 0, out_dim).reshape(wide_out)
+
+
+def _press_points(packet, named_axis, here_x, frame_in):
+    earlier, outcome_arr = (lax.axis_size(named_axis), lax.axis_index(named_axis))
+    v_now = _remake_run(packet, here_x, earlier)
+    seen = [v_now[outcome_arr]]
+    for ii in tuple(range(1, earlier)):
+        v1 = v_now[(outcome_arr + ii) % earlier]
+        seen.append(
+            lax.ppermute(v1, named_axis, [(rr, (rr + ii) % earlier) for rr in range(earlier)])
+        )
+    v_now = jnp.stack(seen)[(outcome_arr - jnp.arange(earlier)) % earlier]
+    return _clear_levels_all(v_now, frame_in)
+
+
+step_on_space_all = functools.partial(_press_points, named_axis="pix", here_x=0, frame_in=2)
 
 
 def with_halo(block, sides, width):
@@ -117,7 +149,7 @@
     pix_count = lax.axis_size("pix")
     per_device = frames_here // pix_count
     grouped = temporal_rows.reshape(pix_count, per_device, pixel_count, channels)
-    frame_block = lax.all_to_all(grouped, "pix", split_axis=0, concat_axis=2, tiled=True)[0]
+    frame_block = step_on_space_all(grouped)[0]
     result = lax.map(
         lambda frame_rows: spatial_frame(frame_rows, spatial_gain, spatial_qkv, spatial_out),
         frame_block,

time: 77.9 us -> 73.7 us (0.946)
  waiting for transfers between devices: 7.37 us -> 3.25 us
    all_to_all x1 -> x0, waiting for transfers between devices: 7.37 us -> none  [body(): lax.all_to_all(grouped, 'pix', split_axis=0, concat_axis=2, tiled=True)[0]]
    all_to_all x1 -> x0, starting transfers between devices: 3.46 us -> none  [body(): lax.all_to_all(grouped, 'pix', split_axis=0, concat_axis=2, tiled=True)[0]]
    ppermute x0 -> x3, waiting for transfers between devices: none -> 3.25 us  [_press_points(): lax.ppermute(v1, named_axis, [(rr, (rr + ii) % earlier) for rr in range(e...]
    ppermute x0 -> x3, starting transfers between devices: none -> 3 us  [_press_points(): lax.ppermute(v1, named_axis, [(rr, (rr + ii) % earlier) for rr in range(e...]
  transfers between devices with their start and end apart: 3 -> 5, of which waited for: 1 -> 3; matrix products, arithmetic and copies ran while one was open for 5% -> 5% of each run, Pallas kernels for 0% -> 0%
where the time goes in v1:
time: 73.7 us; the launch traced here: 72.9 us
  local copies, waits for them, and re-layouts  18.6 us (25%)
  blocking collectives  16.6 us (23%)
  matrix products  14.2 us (19%)
  other arithmetic  9.6 us (13%)
  starting transfers between devices  9.25 us (13%)
  waiting for transfers between devices  3.25 us (4%)
  between operations  1 us (1%)
    all_gather x1, blocking collectives, body(): lax.all_gather(picked, 'clip', axis=0, tiled=True)  16.6 us
    ppermute x1, starting transfers between devices, with_halo(): lax.ppermute(lax.slice_in_dim(block, block.shape[dim] - width, None, axis...  4.96 us
    reshape x2, local copies, waits for them, and re-layouts, project(): return result.reshape(shape[:-1] + (matrix.shape[1],))  4.31 us
    reshape x1, local copies, waits for them, and re-layouts, temporal_attend(): values = key_pairs[..., channels:].reshape(depth, pixels, HEADS, HEAD_DIM)  3.85 us
    concatenate x1, other arithmetic, body(): jnp.concatenate([border, global_pairs], 0)  3.64 us
    ppermute x3, waiting for transfers between devices, _press_points(): lax.ppermute(v1, named_axis, [(rr, (rr + ii) % earlier) for rr in range(e...  3.25 us
    ppermute x3, starting transfers between devices, _press_points(): lax.ppermute(v1, named_axis, [(rr, (rr + ii) % earlier) for rr in range(e...  3 us
    reshape x1, local copies, waits for them, and re-layouts, temporal_attend(): keys = key_pairs[..., :channels].reshape(depth, pixels, HEADS, HEAD_DIM)  2.93 us
  transfers between devices with their start and end apart: 5, of which 3 were waited for; matrix products, arithmetic and copies ran while one was open for 5% of the time, Pallas kernels for 0%

profile of v1, /device:TPU:0, one launch (start us, length us, event | category | flops | bytes accessed | tf_op | source)
XLA Modules:
  0.0 72.9 jit_solution(12725626316418151524)
XLA Ops:
  0.0 1.2 %convert_reduce_fusion.1 = f32[8,64]{1,0:T(8,128)S(1)} fusion(bf16[8,64,320]{2,1,0:T(8,128)(2,1)} %param.12), kind=kLoop, calls=%fused_computation.60 | loop fusion | flops 327168 | bytes 329728 | tf_op jit(solution)/shard_map/reduce_sum | solution.py:59
  1.2 1.3 %multiply_reduce_fusion = f32[8,64]{1,0:T(8,128)S(1)} fusion(bf16[8,64,320]{2,1,0:T(8,128)(2,1)} %param.12, f32[8,64]{1,0:T(8,128)S(1)} %broadcast_multiply_fusion.1), kind=kLoop, calls=%fused_computation.58 | loop fusion | flops 654848 | bytes 331776 | tf_op jit(solution)/shard_map/reduce_sum | solution.py:61
  2.5 1.2 %multiply_convert_fusion = bf16[8,64,320]{2,1,0:T(8,128)(2,1)S(1)} fusion(bf16[8,64,320]{2,1,0:T(8,128)(2,1)} %param.12, f32[320]{0:T(512)} %param.14, f32[8,64]{1,0:T(8,128)S(1)} %add_rsqrt_fusion.1, f32[8,64]{1,0:T(8,128)S(1)} %broadcast_multiply_fusion.1), kind=kLoop, calls=%fused_computation.57 | loop fusion | flops 819200 | bytes 660736 | tf_op jit(solution)/shard_map/convert_element_type | solution.py:62
  3.7 0.8 %fusion.40 = (bf16[4,64,320]{2,1,0:T(8,128)(2,1)}, bf16[4,64,320]{2,1,0:T(8,128)(2,1)}) fusion(bf16[8,64,320]{2,1,0:T(8,128)(2,1)S(1)} %multiply_convert_fusion), kind=kLoop, calls=%fused_computation.81 | loop fusion | bytes 655360 | tf_op jit(solution)/shard_map/slice | solution.py:50
  4.5 5.0 %collective-permute-start = (bf16[4,64,320]{2,1,0:T(8,128)(2,1)}, bf16[4,64,320]{2,1,0:T(8,128)(2,1)S(1)}, u32[]{:S(2)}, u32[]{:S(2)}) collective-permute-start(bf16[4,64,320]{2,1,0:T(8,128)(2,1)} %get-tuple-element.125), channel_id=1, source_target_pairs={{0,4},{4,8},{8,12},{1,5},{5,9},{9,13},{2,6},{6,10},{10,14},{3,7},{... | collective-permute-start | bytes 491528 | tf_op jit(solution)/shard_map/ppermute | solution.py:49
  9.5 1.3 %collective-permute-start.1 = (bf16[4,64,320]{2,1,0:T(8,128)(2,1)}, bf16[4,64,320]{2,1,0:T(8,128)(2,1)}, u32[]{:S(2)}, u32[]{:S(2)}) collective-permute-start(bf16[4,64,320]{2,1,0:T(8,128)(2,1)} %get-tuple-element.126), channel_id=1, source_target_pairs={{4,0},{8,4},{12,8},{5,1},{9,5},{13,9},{6,2},{10,6},{14,10},{7,3},{... | collective-permute-start | bytes 491528 | tf_op jit(solution)/shard_map/ppermute | solution.py:52
  11.5 16.6 %all_gather.3 = bf16[4,64,320]{2,1,0:T(8,128)(2,1)S(1)} all-gather(bf16[1,64,320]{2,1,0:T(8,128)(2,1)S(1)} %constant_dynamic-slice_fusion.1), channel_id=1, replica_groups=mesh['group'=2,'clip'=4,'pix'=4] {'clip'}, dimensions={0}, use_global_device_ids=true | all-gather | bytes 204800 | tf_op jit(solution)/shard_map/all_gather | solution.py:132
  29.0 1.1 %copy.26 = bf16[4,64,640]{1,2,0:T(8,128)(2,1)} copy(bf16[4,64,640]{2,1,0:T(8,128)(2,1)S(1)} %bitcast.141) | data formatting | bytes 655360 | tf_op jit(solution)/shard_map/reshape | solution.py:69
  30.4 0.6 copy.27
  31.0 1.0 %copy.31 = f32[512,320]{0,1:T(8,128)} copy(bf16[512,320]{1,0:T(8,128)(2,1)S(1)} %bitcast.134) | data formatting | bytes 983040 | tf_op jit(solution)/shard_map/reshape | solution.py:146
  32.1 1.1 %pad_maximum_fusion.1 = bf16[16,64,320]{2,1,0:T(8,128)(2,1)S(1)} fusion(bf16[4,64,320]{2,1,0:T(8,128)(2,1)} %collective-permute-done.1, bf16[8,64,320]{2,1,0:T(8,128)(2,1)S(1)} %multiply_convert_fusion, bf16[4,64,320]{2,1,0:T(8,128)(2,1)S(1)} %collective-permute-done), kind=kLoop, calls=%fused_computation.56 | loop fusion | flops 655360 | bytes 1310720 | tf_op jit(solution)/shard_map/concatenate | solution.py:53
  33.2 2.0 %convolution_convert_fusion.2 = bf16[1024,640]{1,0:T(8,128)(2,1)} fusion(bf16[1024,320]{1,0:T(8,128)(2,1)S(1)} %bitcast.137, bf16[320,960]{1,0:T(8,128)(2,1)S(1)} %copy-done.5), kind=kOutput, calls=%fused_computation.44 | convolution fusion | flops 420085760 | bytes 2506752 | tf_op jit(solution)/shard_map/dot_general | solution.py:68
  35.2 3.2 %copy.25 = bf16[16,64,640]{1,2,0:T(8,128)(2,1)S(1)} copy(bf16[16,64,640]{2,1,0:T(8,128)(2,1)} %bitcast.135) | data formatting | bytes 2621440 | tf_op jit(solution)/shard_map/reshape | solution.py:69
  38.4 3.6 %pad_maximum_fusion = (bf16[20,64,320]{1,2,0:T(8,128)(2,1)}, bf16[20,64,320]{1,2,0:T(8,128)(2,1)}) fusion(bf16[4,64,640]{1,2,0:T(8,128)(2,1)} %copy.26, bf16[16,64,640]{1,2,0:T(8,128)(2,1)S(1)} %copy.25), kind=kLoop, calls=%fused_computation.43 | loop fusion | flops 3276800 | bytes 3276800 | tf_op jit(solution)/shard_map/concatenate | solution.py:142
  42.1 2.9 %copy.28 = bf16[20,64,5,64]{3,0,2,1:T(8,128)(2,1)S(1)} copy(bf16[20,64,5,64]{1,3,2,0:T(8,128)(2,1)} %bitcast.133) | data formatting | bytes 1638400 | tf_op jit(solution)/shard_map/reshape | solution.py:75
  45.0 3.9 %copy.29 = bf16[20,64,5,64]{3,0,2,1:T(8,128)(2,1)} copy(bf16[20,64,5,64]{1,3,2,0:T(8,128)(2,1)} %bitcast.132) | data formatting | bytes 1638400 | tf_op jit(solution)/shard_map/reshape | solution.py:76
  48.9 2.3 %fusion.41 = (f32[64,5,8]{2,1,0:T(8,128)S(1)}, f32[64,5,8,20]{3,2,1,0:T(8,128)}) fusion(bf16[8,64,5,64]{3,0,2,1:T(8,128)(2,1)S(1)} %copy.27, bf16[20,64,5,64]{3,0,2,1:T(8,128)(2,1)S(1)} %copy.28, pred[20]{0:T(512)(128)(4,1)S(1)} %concatenate.11), kind=kOutput, calls=%fused_computation.82 | convolution fusion | flops 6758419 | bytes 1361940 | tf_op jit(solution)/shard_map/sub | solution.py:83
  51.2 2.7 %fusion.31 = bf16[8,64,5,64]{3,0,2,1:T(8,128)(2,1)S(1)} fusion(bf16[20,64,5,64]{3,0,2,1:T(8,128)(2,1)} %copy.29, f32[64,5,8,20]{3,2,1,0:T(8,128)} %get-tuple-element.128, f32[64,5,8]{2,1,0:T(8,128)S(1)} %get-tuple-element.127), kind=kOutput, calls=%fused_computation.51 | convolution fusion | flops 6819840 | bytes 1361920 | tf_op jit(solution)/shard_map/phfk,kphd->fphd/dot_general | solution.py:85
  53.9 0.6 copy.30
  55.7 1.6 %collective-permute-start.3 = (bf16[1,2,64,320]{3,2,1,0:T(8,128)(2,1)S(1)}, bf16[1,2,64,320]{3,2,1,0:T(8,128)(2,1)S(1)}, u32[]{:S(2)}, u32[]{:S(2)}) collective-permute-start(bf16[1,2,64,320]{3,2,1,0:T(8,128)(2,1)S(1)} %get-tuple-element.123), channel_id=1, source_target_pairs={{0,2},{1,3},{2,0},{3,1},{4,6},{5,7},{6,4},{7,5},{8,10},{9,11},{10,... | collective-permute-start | bytes 245768 | tf_op jit(solution)/shard_map/ppermute | solution.py:35
  57.3 1.4 %collective-permute-start.4 = (bf16[1,2,64,320]{3,2,1,0:T(8,128)(2,1)S(1)}, bf16[1,2,64,320]{3,2,1,0:T(8,128)(2,1)S(1)}, u32[]{:S(2)}, u32[]{:S(2)}) collective-permute-start(bf16[1,2,64,320]{3,2,1,0:T(8,128)(2,1)S(1)} %get-tuple-element.122), channel_id=1, source_target_pairs={{0,3},{1,0},{2,1},{3,2},{4,7},{5,4},{6,5},{7,6},{8,11},{9,8},{10,9... | collective-permute-start | bytes 245768 | tf_op jit(solution)/shard_map/ppermute | solution.py:35
  58.7 1.5 %collective-permute-done.2 = bf16[1,2,64,320]{3,2,1,0:T(8,128)(2,1)S(1)} collective-permute-done((bf16[1,2,64,320]{3,2,1,0:T(8,128)(2,1)S(1)}, bf16[1,2,64,320]{3,2,1,0:T(8,128)(2,1)S(1)}, u32[]{:S(2)}, u32[]{:S(2)}) %collective-permute-start.2) | collective-permute-done | bytes 81952 | tf_op jit(solution)/shard_map/ppermute | solution.py:35
  60.1 1.3 %collective-permute-done.3 = bf16[1,2,64,320]{3,2,1,0:T(8,128)(2,1)S(1)} collective-permute-done((bf16[1,2,64,320]{3,2,1,0:T(8,128)(2,1)S(1)}, bf16[1,2,64,320]{3,2,1,0:T(8,128)(2,1)S(1)}, u32[]{:S(2)}, u32[]{:S(2)}) %collective-permute-start.3) | collective-permute-done | bytes 81952 | tf_op jit(solution)/shard_map/ppermute | solution.py:35
  62.0 0.6 gather_fusion
  62.9 10.0 %while.25 = (s32[]{:T(128)}, bf16[2,256,320]{1,2,0:T(8,128)(2,1)}, bf16[2,256,320]{1,2,0:T(8,128)(2,1)S(1)}, f32[320]{0:T(512)S(1)}, bf16[320,960]{1,0:T(8,128)(...) while((s32[]{:T(128)}, bf16[2,256,320]{1,2,0:T(8,128)(2,1)}, ...), condition=%wide.region_11.12_spmd, body=%wide.region_4.11_spmd.sunk | while | flops 228359936 | bytes 7997730 | solution.py:153
  63.1 0.5 convolution_convert_fusion.7
  63.7 0.5 copy.36
  64.2 2.6 %while.26 = (s32[]{:T(128)}, bf16[5,256,64]{1,2,0:T(8,128)(2,1)S(1)}, bf16[5,256,64]{2,1,0:T(8,128)(2,1)S(1)}, bf16[5,256,64]{2,1,0:T(8,128)(2,1)S(1)}, bf16[5,256,64]{2,1,0:T(8,128)(2,1)S(1)}, /*index=5*/s32[]{:T(128)}) while((s32[]{:T(128)}, bf16[5,256,64]{1,2,0:T(8,128)(2,1)S(1)}, bf16[5,256,64]{2,1,0:T(8,128)(2,1)S(1)}, ...), condition=%wide.region_10.10_spmd, body=%wide.region_7.9_spmd.sunk | while | flops 17251840 | bytes 1023045 | solution.py:111
  67.2 0.7 copy-done.8
  68.1 0.5 convolution_convert_fusion.7
  69.2 2.6 %while.26 = (s32[]{:T(128)}, bf16[5,256,64]{1,2,0:T(8,128)(2,1)S(1)}, bf16[5,256,64]{2,1,0:T(8,128)(2,1)S(1)}, bf16[5,256,64]{2,1,0:T(8,128)(2,1)S(1)}, bf16[5,256,64]{2,1,0:T(8,128)(2,1)S(1)}, /*index=5*/s32[]{:T(128)}) while((s32[]{:T(128)}, bf16[5,256,64]{1,2,0:T(8,128)(2,1)S(1)}, bf16[5,256,64]{2,1,0:T(8,128)(2,1)S(1)}, ...), condition=%wide.region_10.10_spmd, body=%wide.region_7.9_spmd.sunk | while | flops 17251840 | bytes 1023045 | solution.py:111
  72.2 0.7 copy-done.8
  (87 shorter events, 9.8 us)
Async XLA Ops:
  0.0 54.9 %copy-start = (bf16[320,320]{1,0:T(8,128)(2,1)S(1)}, bf16[320,320]{1,0:T(8,128)(2,1)}, u32[]{:S(2)}) copy-start(bf16[320,320]{1,0:T(8,128)(2,1)} %param.16) | copy-start | bytes 614404
  0.0 28.1 %copy-start.5 = (bf16[320,960]{1,0:T(8,128)(2,1)S(1)}, bf16[320,960]{1,0:T(8,128)(2,1)}, u32[]{:S(2)}) copy-start(bf16[320,960]{1,0:T(8,128)(2,1)} %param.15) | copy-start | bytes 1843204
  4.5 27.5 %collective-permute-start = (bf16[4,64,320]{2,1,0:T(8,128)(2,1)}, bf16[4,64,320]{2,1,0:T(8,128)(2,1)S(1)}, u32[]{:S(2)}, u32[]{:S(2)}) collective-permute-start(bf16[4,64,320]{2,1,0:T(8,128)(2,1)} %get-tuple-element.125), channel_id=1, source_target_pairs={{0,4},{4,8},{8,12},{1,5},{5,9},{9,13},{2,6},{6,10},{10,14},{3,7},{... | collective-permute-start | bytes 491528 | tf_op jit(solution)/shard_map/ppermute | solution.py:49
  9.5 22.6 %collective-permute-start.1 = (bf16[4,64,320]{2,1,0:T(8,128)(2,1)}, bf16[4,64,320]{2,1,0:T(8,128)(2,1)}, u32[]{:S(2)}, u32[]{:S(2)}) collective-permute-start(bf16[4,64,320]{2,1,0:T(8,128)(2,1)} %get-tuple-element.126), channel_id=1, source_target_pairs={{4,0},{8,4},{12,8},{5,1},{9,5},{13,9},{6,2},{10,6},{14,10},{7,3},{... | collective-permute-start | bytes 491528 | tf_op jit(solution)/shard_map/ppermute | solution.py:52
  29.0 2.0 %copy-start.2 = (bf16[8,64,320]{2,1,0:T(8,128)(2,1)S(1)}, bf16[8,64,320]{2,1,0:T(8,128)(2,1)}, u32[]{:S(2)}) copy-start(bf16[8,64,320]{2,1,0:T(8,128)(2,1)} %param.12) | copy-start | bytes 983044
  53.9 1.1 %copy-start.4 = (f32[512,320]{0,1:T(8,128)S(1)}, f32[512,320]{0,1:T(8,128)}, u32[]{:S(2)}) copy-start(f32[512,320]{0,1:T(8,128)} %copy.31) | copy-start | bytes 1966084
  55.6 7.3 %copy-start.1 = (bf16[320,960]{1,0:T(8,128)(2,1)S(1)}, bf16[320,960]{1,0:T(8,128)(2,1)}, u32[]{:S(2)}) copy-start(bf16[320,960]{1,0:T(8,128)(2,1)} %param.18) | copy-start | bytes 1843204
  55.6 7.3 %copy-start.3 = (bf16[320,320]{1,0:T(8,128)(2,1)S(1)}, bf16[320,320]{1,0:T(8,128)(2,1)}, u32[]{:S(2)}) copy-start(bf16[320,320]{1,0:T(8,128)(2,1)} %param.19) | copy-start | bytes 614404
  55.6 7.3 %copy-start.6 = (f32[320]{0:T(512)S(1)}, f32[320]{0:T(512)}, u32[]{:S(2)}) copy-start(f32[320]{0:T(512)} %param.17) | copy-start | bytes 3844
  55.7 4.5 %collective-permute-start.2 = (bf16[1,2,64,320]{3,2,1,0:T(8,128)(2,1)S(1)}, bf16[1,2,64,320]{3,2,1,0:T(8,128)(2,1)S(1)}, u32[]{:S(2)}, u32[]{:S(2)}) collective-permute-start(bf16[1,2,64,320]{3,2,1,0:T(8,128)(2,1)S(1)} %get-tuple-element.124), channel_id=1, source_target_pairs={{0,1},{1,2},{2,3},{3,0},{4,5},{5,6},{6,7},{7,4},{8,9},{9,10},{10,1... | collective-permute-start | bytes 245768 | tf_op jit(solution)/shard_map/ppermute | solution.py:35
  55.7 5.7 %collective-permute-start.3 = (bf16[1,2,64,320]{3,2,1,0:T(8,128)(2,1)S(1)}, bf16[1,2,64,320]{3,2,1,0:T(8,128)(2,1)S(1)}, u32[]{:S(2)}, u32[]{:S(2)}) collective-permute-start(bf16[1,2,64,320]{3,2,1,0:T(8,128)(2,1)S(1)} %get-tuple-element.123), channel_id=1, source_target_pairs={{0,2},{1,3},{2,0},{3,1},{4,6},{5,7},{6,4},{7,5},{8,10},{9,11},{10,... | collective-permute-start | bytes 245768 | tf_op jit(solution)/shard_map/ppermute | solution.py:35
  57.3 4.6 %collective-permute-start.4 = (bf16[1,2,64,320]{3,2,1,0:T(8,128)(2,1)S(1)}, bf16[1,2,64,320]{3,2,1,0:T(8,128)(2,1)S(1)}, u32[]{:S(2)}, u32[]{:S(2)}) collective-permute-start(bf16[1,2,64,320]{3,2,1,0:T(8,128)(2,1)S(1)} %get-tuple-element.122), channel_id=1, source_target_pairs={{0,3},{1,0},{2,1},{3,2},{4,7},{5,4},{6,5},{7,6},{8,11},{9,8},{10,9... | collective-permute-start | bytes 245768 | tf_op jit(solution)/shard_map/ppermute | solution.py:35
  64.2 2.7 %copy-start.7 = (bf16[2,256,320]{1,2,0:T(8,128)(2,1)S(1)}, bf16[2,256,320]{1,2,0:T(8,128)(2,1)}, u32[]{:S(2)}) copy-start(bf16[2,256,320]{1,2,0:T(8,128)(2,1)} %get-tuple-element.248) | copy-start | bytes 983044 | tf_op jit(solution)/shard_map/while
  67.2 0.7 copy-start.8
  69.2 2.7 %copy-start.7 = (bf16[2,256,320]{1,2,0:T(8,128)(2,1)S(1)}, bf16[2,256,320]{1,2,0:T(8,128)(2,1)}, u32[]{:S(2)}) copy-start(bf16[2,256,320]{1,2,0:T(8,128)(2,1)} %get-tuple-element.248) | copy-start | bytes 983044 | tf_op jit(solution)/shard_map/while
  72.2 0.7 copy-start.8
